TPU v7x, 256 devices: a whole 4x4x8 slice. The times are simulated.
256 devices in a mesh: row: 16 (over y, z_lo, core), col: 16 (over z_hi, x).
Axes of the slice: x: 4, y: 4, z: 8 (z_hi: 4, z_lo: 2; z = z_hi * 2 + z_lo), core: 2. Of those that a mesh axis runs over, the one named last changes fastest.
Arguments:
- pairs: bfloat16 [2, 256, 20480], P(None, None, ('row', 'col')), may hold values from -12 to 12
- prior: bfloat16 [2, 20480, 20480], P(None, 'row', 'col'), may hold values from -0.025146484 to 0.025146484
- val_band: int32 [256], replicated, may hold values from 0 to 255
- cond_band: int32 [256], replicated, may hold values from 0 to 2047
- val_energy: float32 [256], replicated, may hold values from -3 to -1
- cond_energy: float32 [2048], replicated, may hold values from 0.5 to 2.5
- coul_root: float32 [20480], replicated, may hold values from 0.3 to 1.5
- potential: float32 [2, 128, 20480], P(None, 'col', 'row'), may hold values from -6 to 6
Outputs:
- screened: float32 [2, 128, 20480], P(None, 'col', 'row')
All inputs are finite; a program needn't handle non-finite values.
Results may differ from a plain program's by a relative error of at most 0.0007.
Values may be sent and summed in bfloat16 or wider, within the bound.
No kernel may reach another device: no remote copies, remote signals or barrier semaphores. Data moves between devices by JAX's collectives and lax.ppermute only.
A program may use at most 128 MiB of HBM per device.

v0:
```python
import jax
import jax.numpy as jnp
from jax import lax
from jax.sharding import PartitionSpec as P

NG = 20480
ITERS = 2


def spread(block, axis, holder):
    block = jnp.where(lax.axis_index(axis) == holder, block, jnp.zeros_like(block))
    return lax.psum(block, axis)


def contract_pairs(first, second):
    return lax.dot_general(
        first, second, (((0,), (0,)), ((), ())), preferred_element_type=jnp.float32
    )


def through(scaled_part, matrix):
    return lax.dot_general(
        scaled_part,
        matrix,
        (((1,), (1,)), ((), ())),
        precision=lax.Precision.HIGHEST,
        preferred_element_type=jnp.float32,
    )


def pick_energy(band, energy):
    levels = jnp.arange(energy.shape[0], dtype=jnp.int32)
    return jnp.sum(jnp.where(band[:, None] == levels[None, :], energy[None, :], 0.0), axis=1)


def column_values(gathered, gain_row, source_row):
    scaled = gathered * gain_row[None, None, :]
    return spread(scaled, "row", source_row)


def respond(scaled_cols, response_real, response_imag):
    real_part = through(scaled_cols[0], response_real) - through(scaled_cols[1], response_imag)
    imag_part = through(scaled_cols[0], response_imag) + through(scaled_cols[1], response_real)
    return jnp.stack([real_part, imag_part])


def local(pairs, prior, val_band, cond_band, val_energy, cond_energy, coul_root, potential):
    row_count = lax.axis_size("row")
    col_count = lax.axis_size("col")
    row_index = lax.axis_index("row")
    col_index = lax.axis_index("col")
    row_width = prior.shape[1]
    source_row = col_index * row_count // col_count
    weights = 1.0 / (pick_energy(cond_band, cond_energy) - pick_energy(val_band, val_energy))
    row_pairs = lax.all_gather(pairs, "col", axis=2, tiled=True)
    col_pairs = spread(row_pairs, "row", source_row)
    weighted = (weights[None, :, None] * col_pairs.astype(jnp.float32)).astype(jnp.bfloat16)
    left_stack = jnp.concatenate([row_pairs[0], row_pairs[1]], axis=0)
    right_stack = jnp.concatenate([weighted[0], weighted[1]], axis=0)
    response_real = prior[0].astype(jnp.float32) + contract_pairs(left_stack, right_stack) / NG
    left_other = jnp.concatenate([row_pairs[0], -row_pairs[1]], axis=0)
    right_other = jnp.concatenate([weighted[1], weighted[0]], axis=0)
    response_imag = prior[1].astype(jnp.float32) + contract_pairs(left_other, right_other) / NG
    gain_row = lax.dynamic_slice_in_dim(coul_root, row_index * row_width, row_width, 0)
    iterate = potential
    for _ in range(ITERS):
        gathered = lax.all_gather(iterate, "col", axis=1, tiled=True)
        scaled_cols = column_values(gathered, gain_row, source_row)
        partial_value = respond(scaled_cols, response_real, response_imag)
        summed = lax.psum_scatter(partial_value, "col", scatter_dimension=1, tiled=True)
        applied = iterate + gain_row[None, None, :] * summed
        iterate = iterate + 0.5 * (potential - applied)
    return iterate


def solution(mesh):
    in_specs = (
        P(None, None, ("row", "col")),
        P(None, "row", "col"),
        P(),
        P(),
        P(),
        P(),
        P(),
        P(None, "col", "row"),
    )
    out_specs = P(None, "col", "row")
    return jax.shard_map(local, mesh=mesh, in_specs=in_specs, out_specs=out_specs, check_vma=False)
```

profile of v0, /device:TPU:8, one launch (start us, length us, event | category | flops | bytes accessed | tf_op | source)
XLA Modules:
  0.0 811.0 jit_solution(6735044136014977329)
XLA Ops:
  6.5 0.0 all-gather.6.cloned.1.call-start
  6.5 0.7 all-gather.6.cloned.1.call-update
  7.3 0.0 all-gather.4.cloned.1.call-start
  7.3 0.7 all-gather.4.cloned.1.call-update
  8.0 0.0 all-reduce.6.cloned.1.call-start
  8.1 58.8 %all-gather.6.cloned.1.call-done = bf16[2,256,1280]{1,2,0:T(8,128)(2,1)} async-done(((bf16[2,256,80]{1,2,0:T(8,128)(2,1)}), bf16[2,256,1280]{1,2,0:T(8,128)(2,1)}) %all-gather.6.cloned.1.call-update) | async-done | bytes 1310736 | tf_op jit(solution)/shard_map/all_gather | solution.py:55
  66.9 1.2 broadcast_select_fusion
  68.1 0.0 all-reduce.6.cloned.1.call-update
  68.1 0.0 all-reduce.4.cloned.1.call-start
  68.2 0.8 dynamic_slice.3
  69.0 0.0 copy-done.7
  69.0 0.0 copy-done.8
  69.0 0.2 select_reduce_fusion.1
  69.2 0.0 copy-done.6
  69.2 0.0 copy-done.9
  69.2 0.4 select_reduce_fusion
  69.6 51.5 %all-gather.4.cloned.1.call-done = f32[2,128,1280]{2,1,0:T(8,128)} async-done(((f32[2,8,1280]{2,1,0:T(8,128)}), f32[2,128,1280]{2,1,0:T(8,128)}) %all-gather.4.cloned.1.call-update) | async-done | bytes 1310736 | tf_op jit(solution)/shard_map/all_gather | solution.py:67
  121.1 2.5 multiply_select_fusion.1
  123.5 0.0 all-reduce.4.cloned.1.call-update
  123.6 0.0 reduce-scatter.3.cloned.1.call-start
  123.6 1.2 copy-done.1
  124.9 0.1 slice_bitcast_fusion.5
  125.0 116.9 %all-reduce.6.cloned.1.call-done = bf16[2,256,1280]{1,2,0:T(8,128)(2,1)} async-done(((bf16[2,256,1280]{1,2,0:T(8,128)(2,1)}), bf16[2,256,1280]{1,2,0:T(8,128)(2,1)}) %all-reduce.6.cloned.1.call-update) | async-done | bytes 1310736 | tf_op jit(solution)/shard_map/psum | solution.py:12
  241.9 1.6 multiply_convert_fusion
  243.5 0.0 slice-start.4
  243.5 0.1 slice_bitcast_fusion.3
  243.6 0.0 slice-start.5
  243.6 6.7 fusion.1
  250.3 0.0 slice-done.4
  250.3 0.0 slice-done.5
  250.3 4.7 fusion
  255.0 115.7 %all-reduce.4.cloned.1.call-done = f32[2,128,1280]{2,1,0:T(8,128)} async-done(((f32[2,128,1280]{2,1,0:T(8,128)}), f32[2,128,1280]{2,1,0:T(8,128)}) %all-reduce.4.cloned.1.call-update) | async-done | bytes 1310736 | tf_op jit(solution)/shard_map/psum | solution.py:12
  370.7 9.9 %fusion.14 = f32[128,1280]{1,0:T(8,128)S(1)} fusion(f32[1280,1280]{1,0:T(8,128)} %fusion.1, f32[2,128,1280]{2,1,0:T(8,128)} %all-reduce.4.cloned.1.call-done), kind=kOutput, calls=%fused_computation.38 | convolution fusion | flops 2516582400 | bytes 7864320 | tf_op jit(solution)/shard_map/dot_general | solution.py:22
  380.6 0.0 copy-done
  380.7 0.0 copy-done.2
  380.7 0.0 slice-start
  380.7 6.9 fusion.15
  387.6 0.0 slice-start.1
  387.6 6.8 fusion.3
  394.4 7.0 fusion.2
  401.4 1.1 pad_maximum_fusion.4
  402.6 0.0 reduce-scatter.3.cloned.1.call-update
  402.6 0.0 all-gather.8.cloned.1.call-start
  402.7 93.3 %reduce-scatter.3.cloned.1.call-done = f32[2,8,1280]{2,1,0:T(8,128)} async-done(((f32[2,128,1280]{2,1,0:T(8,128)}), f32[2,8,1280]{2,1,0:T(8,128)}) %reduce-scatter.3.cloned.1.call-update) | async-done | bytes 81936 | tf_op jit(solution)/shard_map/reduce_scatter | solution.py:70
  496.0 0.0 copy-done.4
  496.0 1.5 fusion.19
  497.5 0.0 all-gather.8.cloned.1.call-update
  497.6 0.0 all-reduce.8.cloned.1.call-start
  497.6 52.5 %all-gather.8.cloned.1.call-done = f32[2,128,1280]{2,1,0:T(8,128)} async-done(((f32[2,8,1280]{2,1,0:T(8,128)}), f32[2,128,1280]{2,1,0:T(8,128)}) %all-gather.8.cloned.1.call-update) | async-done | bytes 1310736 | tf_op jit(solution)/shard_map/all_gather | solution.py:67
  550.1 2.5 multiply_select_fusion
  552.6 0.0 all-reduce.8.cloned.1.call-update
  552.6 0.0 reduce-scatter.5.cloned.1.call-start
  552.7 118.3 %all-reduce.8.cloned.1.call-done = f32[2,128,1280]{2,1,0:T(8,128)} async-done(((f32[2,128,1280]{2,1,0:T(8,128)}), f32[2,128,1280]{2,1,0:T(8,128)}) %all-reduce.8.cloned.1.call-update) | async-done | bytes 1310736 | tf_op jit(solution)/shard_map/psum | solution.py:12
  671.0 9.9 %fusion.16 = f32[128,1280]{1,0:T(8,128)S(1)} fusion(f32[1280,1280]{1,0:T(8,128)} %fusion.1, f32[2,128,1280]{2,1,0:T(8,128)} %all-reduce.8.cloned.1.call-done), kind=kOutput, calls=%fused_computation.40 | convolution fusion | flops 2516582400 | bytes 7864320 | tf_op jit(solution)/shard_map/dot_general | solution.py:22
  680.9 0.0 slice-start.2
  680.9 9.8 %fusion.17 = f32[128,1280]{1,0:T(8,128)S(1)} fusion(f32[1280,1280]{1,0:T(8,128)} %fusion, f32[2,128,1280]{2,1,0:T(8,128)S(1)} %copy-done.3), kind=kOutput, calls=%fused_computation.41 | convolution fusion | flops 2516582400 | bytes 7864320 | tf_op jit(solution)/shard_map/dot_general | solution.py:22
  690.7 0.0 slice-start.3
  690.7 10.0 %fusion.5 = f32[1,128,1280]{2,1,0:T(8,128)S(1)} fusion(f32[128,1280]{1,0:T(8,128)S(1)} %fusion.16, f32[1280,1280]{1,0:T(8,128)} %fusion, f32[2,128,1280]{2,1,0:T(8,128)S(1)} %copy-done.3), kind=kOutput, calls=%fused_computation.12 | convolution fusion | flops 2516746240 | bytes 8519680 | tf_op jit(solution)/shard_map/dot_general | solution.py:22
  700.8 6.8 fusion.4
  707.6 1.2 pad_maximum_fusion.5
  708.7 0.0 reduce-scatter.5.cloned.1.call-update
  708.7 93.4 %reduce-scatter.5.cloned.1.call-done = f32[2,8,1280]{2,1,0:T(8,128)} async-done(((f32[2,128,1280]{2,1,0:T(8,128)}), f32[2,8,1280]{2,1,0:T(8,128)}) %reduce-scatter.5.cloned.1.call-update) | async-done | bytes 81936 | tf_op jit(solution)/shard_map/reduce_scatter | solution.py:70
  802.1 0.0 copy-done.5
  802.1 1.6 multiply_add_fusion
  (20 shorter events, 0.1 us)
Async XLA Ops:
  6.5 60.4 %all-gather.6.cloned.1.call-start = ((), (), s32[]{:S(2)}) async-start(), calls=%async_computation.4 | async-start | bytes 1392640 | tf_op jit(solution)/shard_map/all_gather | solution.py:55
  7.3 113.8 %all-gather.4.cloned.1.call-start = ((), (), s32[]{:S(2)}) async-start(), calls=%async_computation.2 | async-start | bytes 1392640 | tf_op jit(solution)/shard_map/all_gather | solution.py:67
  8.0 233.9 %all-reduce.6.cloned.1.call-start = ((), (), s32[]{:S(2)}) async-start(), calls=%async_computation.5 | async-start | bytes 2621440 | tf_op jit(solution)/shard_map/psum | solution.py:12
  68.1 0.9 copy-start.7
  68.1 0.9 copy-start.8
  68.1 1.1 copy-start.6
  68.1 1.1 copy-start.9
  68.1 302.6 %all-reduce.4.cloned.1.call-start = ((), (), s32[]{:S(2)}) async-start(), calls=%async_computation.3 | async-start | bytes 2621440 | tf_op jit(solution)/shard_map/psum | solution.py:12
  123.5 1.3 copy-start.1
  123.6 372.4 %reduce-scatter.3.cloned.1.call-start = ((), (), s32[]{:S(2)}) async-start(), calls=%async_computation.6 | async-start | bytes 1392640 | tf_op jit(solution)/shard_map/reduce_scatter | solution.py:70
  243.5 6.8 slice-start.4
  243.6 6.7 slice-start.5
  370.7 10.0 %copy-start = (f32[1280,1280]{1,0:T(8,128)S(1)}, f32[1280,1280]{1,0:T(8,128)}, u32[]{:S(2)}) copy-start(f32[1280,1280]{1,0:T(8,128)} %fusion) | copy-start | bytes 19660804
  370.7 10.0 %copy-start.2 = (f32[2,128,1280]{2,1,0:T(8,128)S(1)}, f32[2,128,1280]{2,1,0:T(8,128)}, u32[]{:S(2)}) copy-start(f32[2,128,1280]{2,1,0:T(8,128)} %all-reduce.4.cloned.1.call-done) | copy-start | bytes 3932164
  380.7 13.7 %slice-start = ((s8[6553600]{0:T(1024)(128)(4,1)}), s8[4194304]{0:T(1024)(128)(4,1)S(1)}, s32[]{:S(2)}) async-start(s8[6553600]{0:T(1024)(128)(4,1)} %bitcast.48), calls=%async_computation.10 | async-start | bytes 8388608
  387.6 6.8 slice-start.1
  402.6 93.4 %copy-start.4 = (f32[2,8,1280]{2,1,0:T(8,128)S(1)}, f32[2,8,1280]{2,1,0:T(8,128)}, u32[]{:S(2)}) copy-start(f32[2,8,1280]{2,1,0:T(8,128)} %param.15) | copy-start | bytes 245764
  402.6 147.5 %all-gather.8.cloned.1.call-start = ((), (), s32[]{:S(2)}) async-start(), calls=%async_computation.7 | async-start | bytes 1392640 | tf_op jit(solution)/shard_map/all_gather | solution.py:67
  497.6 173.4 %all-reduce.8.cloned.1.call-start = ((), (), s32[]{:S(2)}) async-start(), calls=%async_computation.8 | async-start | bytes 2621440 | tf_op jit(solution)/shard_map/psum | solution.py:12
  552.6 249.5 %reduce-scatter.5.cloned.1.call-start = ((), (), s32[]{:S(2)}) async-start(), calls=%async_computation.9 | async-start | bytes 1392640 | tf_op jit(solution)/shard_map/reduce_scatter | solution.py:70
  671.0 9.9 %copy-start.3 = (f32[2,128,1280]{2,1,0:T(8,128)S(1)}, f32[2,128,1280]{2,1,0:T(8,128)}, u32[]{:S(2)}) copy-start(f32[2,128,1280]{2,1,0:T(8,128)} %all-reduce.8.cloned.1.call-done) | copy-start | bytes 3932164
  680.9 19.8 %slice-start.2 = ((s8[6553600]{0:T(1024)(128)(4,1)}), s8[4194304]{0:T(1024)(128)(4,1)S(1)}, s32[]{:S(2)}) async-start(s8[6553600]{0:T(1024)(128)(4,1)} %bitcast.50), calls=%async_computation.12 | async-start | bytes 8388608
  690.7 10.1 %slice-start.3 = ((s8[6553600]{0:T(1024)(128)(4,1)}), s8[2359296]{0:T(1024)(128)(4,1)S(1)}, s32[]{:S(2)}) async-start(s8[6553600]{0:T(1024)(128)(4,1)} %bitcast.50), calls=%async_computation.13 | async-start | bytes 4718592
  708.7 93.4 %copy-start.5 = (f32[2,8,1280]{2,1,0:T(8,128)S(1)}, f32[2,8,1280]{2,1,0:T(8,128)}, u32[]{:S(2)}) copy-start(f32[2,8,1280]{2,1,0:T(8,128)} %reduce-scatter.3.cloned.1.call-done) | copy-start | bytes 245764
Sparse Core Ops, SparseCore 0:
  9.8 57.1 all-gather.5
  69.3 51.6 all-gather.3
  123.7 118.1 all-reduce.5
  244.4 126.2 all-reduce.3
  402.7 93.2 reduce-scatter.2
  498.3 51.7 all-gather.7
  552.8 118.1 all-reduce.7
  708.9 93.2 reduce-scatter.4
where the time goes:
time: 820 us; the launch traced here: 811 us
  waiting for transfers between devices  702 us (86%)
  matrix products  78.5 us (10%)
  between operations  14.2 us (2%)
  other arithmetic  13.7 us (2%)
    psum x3, waiting for transfers between devices, spread(): return lax.psum(block, axis)  351 us
    reduce_scatter x2, waiting for transfers between devices, local(): lax.psum_scatter(partial_value, 'col', scatter_dimension=1, tiled=True)  187 us
    all_gather x2, waiting for transfers between devices, local(): gathered = lax.all_gather(iterate, 'col', axis=1, tiled=True)  104 us
    dot_general x8, matrix products, through(): lax.dot_general(scaled_part, matrix, (((1,), (1,)), ((), ())), precision=...  67.1 us
    all_gather x1, waiting for transfers between devices, local(): row_pairs = lax.all_gather(pairs, 'col', axis=2, tiled=True)  58.8 us
  transfers between devices with their start and end apart: 8, of which 8 were waited for; matrix products, arithmetic and copies ran while one was open for 2% of the time, Pallas kernels for 0%

commit v1 on v0

--- a/solution.py
+++ b/solution.py
@@ -64,7 +64,9 @@
     gain_row = lax.dynamic_slice_in_dim(coul_root, row_index * row_width, row_width, 0)
     iterate = potential
     for _ in range(ITERS):
-        gathered = lax.all_gather(iterate, "col", axis=1, tiled=True)
+        gathered = jnp.concatenate(
+            lax.all_to_all(jnp.stack([iterate] * lax.axis_size("col")), "col", 0, 0), axis=1
+        )
         scaled_cols = column_values(gathered, gain_row, source_row)
         partial_value = respond(scaled_cols, response_real, response_imag)
         summed = lax.psum_scatter(partial_value, "col", scatter_dimension=1, tiled=True)

time: 820 us -> 759 us (0.926)
  waiting for transfers between devices: 702 us -> 591 us
  blocking collectives: 0 us -> 38.8 us
  starting transfers between devices: 0.29 us -> 11.2 us
    all_gather x2 -> x0, waiting for transfers between devices: 104 us -> none  [local(): gathered = lax.all_gather(iterate, 'col', axis=1, tiled=True)]
    all_to_all x0 -> x1, blocking collectives: none -> 38.8 us  [local(): lax.all_to_all(jnp.stack([iterate] * lax.axis_size('col')), 'col', 0, 0)]
    all_to_all x0 -> x1, starting transfers between devices: none -> 11 us  [local(): lax.all_to_all(jnp.stack([iterate] * lax.axis_size('col')), 'col', 0, 0)]
  transfers between devices with their start and end apart: 8 -> 7, of which waited for: 8 -> 6; matrix products, arithmetic and copies ran while one was open for 2% -> 3% of each run, Pallas kernels for 0% -> 0%
where the time goes in v1:
time: 759 us; the launch traced here: 749 us
  waiting for transfers between devices  591 us (78%)
  matrix products  78.5 us (10%)
  blocking collectives  38.8 us (5%)
  between operations  14.2 us (2%)
  starting transfers between devices  11.2 us (1%)
  other arithmetic  10.5 us (1%)
    psum x3, waiting for transfers between devices, spread(): return lax.psum(block, axis)  349 us
    reduce_scatter x2, waiting for transfers between devices, local(): lax.psum_scatter(partial_value, 'col', scatter_dimension=1, tiled=True)  187 us
    dot_general x8, matrix products, through(): lax.dot_general(scaled_part, matrix, (((1,), (1,)), ((), ())), precision=...  67.1 us
    all_gather x1, waiting for transfers between devices, local(): row_pairs = lax.all_gather(pairs, 'col', axis=2, tiled=True)  54.7 us
    all_to_all x1, blocking collectives, local(): lax.all_to_all(jnp.stack([iterate] * lax.axis_size('col')), 'col', 0, 0)  38.8 us
  transfers between devices with their start and end apart: 7, of which 6 were waited for; matrix products, arithmetic and copies ran while one was open for 3% of the time, Pallas kernels for 0%

profile of v1, /device:TPU:8, one launch (start us, length us, event | category | flops | bytes accessed | tf_op | source)
XLA Modules:
  0.0 748.9 jit_solution(1501274487878529633)
XLA Ops:
  6.5 0.0 all-gather.2.cloned.1.call-start
  6.5 0.7 all-gather.2.cloned.1.call-update
  7.3 2.1 stack.16
  9.3 11.0 %all-to-all-start = ((f32[16,2,8,1280]{3,2,1,0:T(8,128)}), f32[16,2,8,1280]{3,2,1,0:T(8,128)S(1)}, u32[]{:S(2)}, u32[]{:S(2)}) async-start(f32[16,2,8,1280]{3,2,1,0:T(8,128)} %stack.16), calls=%async_computation | async-start | bytes 2621440 | tf_op jit(solution)/shard_map/all_to_all | solution.py:68
  20.4 0.0 all-reduce.6.cloned.1.call-start
  20.4 54.7 %all-gather.2.cloned.1.call-done = bf16[2,256,1280]{1,2,0:T(8,128)(2,1)} async-done(((bf16[2,256,80]{1,2,0:T(8,128)(2,1)}), bf16[2,256,1280]{1,2,0:T(8,128)(2,1)}) %all-gather.2.cloned.1.call-update) | async-done | bytes 1310736 | tf_op jit(solution)/shard_map/all_gather | solution.py:55
  75.2 1.2 broadcast_select_fusion
  76.4 0.0 all-reduce.6.cloned.1.call-update
  76.4 0.0 all-reduce.4.cloned.1.call-start
  76.4 0.8 dynamic_slice.3
  77.2 0.0 copy-done.7
  77.2 0.0 copy-done.8
  77.2 0.2 select_reduce_fusion.1
  77.4 0.0 copy-done.6
  77.4 0.0 copy-done.9
  77.4 0.4 select_reduce_fusion
  77.8 0.0 all-to-all-done
  77.8 1.2 fusion.15
  79.0 0.0 all-reduce.4.cloned.1.call-update
  79.0 0.0 reduce-scatter.3.cloned.1.call-start
  79.1 1.2 copy-done.1
  80.4 0.1 slice_bitcast_fusion.5
  80.5 115.6 %all-reduce.6.cloned.1.call-done = bf16[2,256,1280]{1,2,0:T(8,128)(2,1)} async-done(((bf16[2,256,1280]{1,2,0:T(8,128)(2,1)}), bf16[2,256,1280]{1,2,0:T(8,128)(2,1)}) %all-reduce.6.cloned.1.call-update) | async-done | bytes 1310736 | tf_op jit(solution)/shard_map/psum | solution.py:12
  196.1 1.6 multiply_convert_fusion
  197.6 0.0 slice-start.4
  197.6 0.1 slice_bitcast_fusion.3
  197.7 0.0 slice-start.5
  197.8 6.7 fusion.1
  204.4 0.0 slice-done.4
  204.5 0.0 slice-done.5
  204.5 4.7 fusion
  209.1 115.9 %all-reduce.4.cloned.1.call-done = f32[2,128,1280]{2,1,0:T(8,128)} async-done(((f32[2,128,1280]{2,1,0:T(8,128)}), f32[2,128,1280]{2,1,0:T(8,128)}) %all-reduce.4.cloned.1.call-update) | async-done | bytes 1310736 | tf_op jit(solution)/shard_map/psum | solution.py:12
  325.0 9.9 %fusion.16 = f32[128,1280]{1,0:T(8,128)S(1)} fusion(f32[1280,1280]{1,0:T(8,128)} %fusion.1, f32[2,128,1280]{2,1,0:T(8,128)} %all-reduce.4.cloned.1.call-done), kind=kOutput, calls=%fused_computation.40 | convolution fusion | flops 2516582400 | bytes 7864320 | tf_op jit(solution)/shard_map/dot_general | solution.py:22
  334.9 0.0 copy-done
  334.9 0.0 copy-done.2
  335.0 0.0 slice-start
  335.0 6.9 fusion.17
  341.9 0.0 slice-start.1
  341.9 6.8 fusion.3
  348.7 0.0 slice-done
  348.7 0.0 slice-done.1
  348.7 7.0 fusion.2
  355.7 1.2 pad_maximum_fusion.4
  356.9 0.0 reduce-scatter.3.cloned.1.call-update
  356.9 0.0 all-reduce.8.cloned.1.call-start
  357.0 93.4 %reduce-scatter.3.cloned.1.call-done = f32[2,8,1280]{2,1,0:T(8,128)} async-done(((f32[2,128,1280]{2,1,0:T(8,128)}), f32[2,8,1280]{2,1,0:T(8,128)}) %reduce-scatter.3.cloned.1.call-update) | async-done | bytes 81936 | tf_op jit(solution)/shard_map/reduce_scatter | solution.py:72
  450.4 0.0 copy-done.4
  450.4 0.9 fusion.21
  451.3 0.1 stack.20
  451.4 38.8 %all_to_all.10 = f32[16,2,8,1280]{3,2,1,0:T(8,128)S(1)} all-to-all(f32[16,2,8,1280]{3,2,1,0:T(8,128)S(1)} %stack.20), channel_id=1, replica_groups=mesh['row'=16,'col'=16] {'col'}, dimensions={0} | all-to-all | bytes 2621440 | tf_op jit(solution)/shard_map/all_to_all | solution.py:68
  490.2 1.2 fusion.14
  491.4 0.0 all-reduce.8.cloned.1.call-update
  491.4 0.0 reduce-scatter.5.cloned.1.call-start
  491.4 117.4 %all-reduce.8.cloned.1.call-done = f32[2,128,1280]{2,1,0:T(8,128)} async-done(((f32[2,128,1280]{2,1,0:T(8,128)}), f32[2,128,1280]{2,1,0:T(8,128)}) %all-reduce.8.cloned.1.call-update) | async-done | bytes 1310736 | tf_op jit(solution)/shard_map/psum | solution.py:12
  608.8 9.9 %fusion.18 = f32[128,1280]{1,0:T(8,128)S(1)} fusion(f32[1280,1280]{1,0:T(8,128)} %fusion.1, f32[2,128,1280]{2,1,0:T(8,128)} %all-reduce.8.cloned.1.call-done), kind=kOutput, calls=%fused_computation.42 | convolution fusion | flops 2516582400 | bytes 7864320 | tf_op jit(solution)/shard_map/dot_general | solution.py:22
  618.7 0.0 slice-start.2
  618.8 9.8 %fusion.19 = f32[128,1280]{1,0:T(8,128)S(1)} fusion(f32[1280,1280]{1,0:T(8,128)} %fusion, f32[2,128,1280]{2,1,0:T(8,128)S(1)} %copy-done.3), kind=kOutput, calls=%fused_computation.43 | convolution fusion | flops 2516582400 | bytes 7864320 | tf_op jit(solution)/shard_map/dot_general | solution.py:22
  628.5 0.0 slice-start.3
  628.5 10.0 %fusion.5 = f32[1,128,1280]{2,1,0:T(8,128)S(1)} fusion(f32[128,1280]{1,0:T(8,128)S(1)} %fusion.18, f32[1280,1280]{1,0:T(8,128)} %fusion, f32[2,128,1280]{2,1,0:T(8,128)S(1)} %copy-done.3), kind=kOutput, calls=%fused_computation.12 | convolution fusion | flops 2516746240 | bytes 8519680 | tf_op jit(solution)/shard_map/dot_general | solution.py:22
  638.6 6.8 fusion.4
  645.4 1.2 pad_maximum_fusion.5
  646.5 0.0 reduce-scatter.5.cloned.1.call-update
  646.6 93.5 %reduce-scatter.5.cloned.1.call-done = f32[2,8,1280]{2,1,0:T(8,128)} async-done(((f32[2,128,1280]{2,1,0:T(8,128)}), f32[2,8,1280]{2,1,0:T(8,128)}) %reduce-scatter.5.cloned.1.call-update) | async-done | bytes 81936 | tf_op jit(solution)/shard_map/reduce_scatter | solution.py:72
  740.0 1.6 multiply_add_fusion
  (19 shorter events, 0.1 us)
Async XLA Ops:
  6.5 68.6 %all-gather.2.cloned.1.call-start = ((), (), s32[]{:S(2)}) async-start(), calls=%async_computation.5 | async-start | bytes 1392640 | tf_op jit(solution)/shard_map/all_gather | solution.py:55
  9.3 68.5 %all-to-all-start = ((f32[16,2,8,1280]{3,2,1,0:T(8,128)}), f32[16,2,8,1280]{3,2,1,0:T(8,128)S(1)}, u32[]{:S(2)}, u32[]{:S(2)}) async-start(f32[16,2,8,1280]{3,2,1,0:T(8,128)} %stack.16), calls=%async_computation | async-start | bytes 2621440 | tf_op jit(solution)/shard_map/all_to_all | solution.py:68
  20.4 175.7 %all-reduce.6.cloned.1.call-start = ((), (), s32[]{:S(2)}) async-start(), calls=%async_computation.6 | async-start | bytes 2621440 | tf_op jit(solution)/shard_map/psum | solution.py:12
  76.3 0.9 copy-start.7
  76.3 0.9 copy-start.8
  76.3 1.1 copy-start.6
  76.3 1.1 copy-start.9
  76.4 248.6 %all-reduce.4.cloned.1.call-start = ((), (), s32[]{:S(2)}) async-start(), calls=%async_computation.4 | async-start | bytes 2621440 | tf_op jit(solution)/shard_map/psum | solution.py:12
  79.0 1.3 copy-start.1
  79.0 371.4 %reduce-scatter.3.cloned.1.call-start = ((), (), s32[]{:S(2)}) async-start(), calls=%async_computation.7 | async-start | bytes 1392640 | tf_op jit(solution)/shard_map/reduce_scatter | solution.py:72
  197.6 6.8 slice-start.4
  197.7 6.7 slice-start.5
  325.0 9.9 %copy-start = (f32[1280,1280]{1,0:T(8,128)S(1)}, f32[1280,1280]{1,0:T(8,128)}, u32[]{:S(2)}) copy-start(f32[1280,1280]{1,0:T(8,128)} %fusion) | copy-start | bytes 19660804
  325.0 10.0 %copy-start.2 = (f32[2,128,1280]{2,1,0:T(8,128)S(1)}, f32[2,128,1280]{2,1,0:T(8,128)}, u32[]{:S(2)}) copy-start(f32[2,128,1280]{2,1,0:T(8,128)} %all-reduce.4.cloned.1.call-done) | copy-start | bytes 3932164
  335.0 13.7 %slice-start = ((s8[6553600]{0:T(1024)(128)(4,1)}), s8[4194304]{0:T(1024)(128)(4,1)S(1)}, s32[]{:S(2)}) async-start(s8[6553600]{0:T(1024)(128)(4,1)} %bitcast.60), calls=%async_computation.10 | async-start | bytes 8388608
  341.9 6.8 slice-start.1
  356.9 93.5 %copy-start.4 = (f32[2,8,1280]{2,1,0:T(8,128)S(1)}, f32[2,8,1280]{2,1,0:T(8,128)}, u32[]{:S(2)}) copy-start(f32[2,8,1280]{2,1,0:T(8,128)} %param.15) | copy-start | bytes 245764
  356.9 251.9 %all-reduce.8.cloned.1.call-start = ((), (), s32[]{:S(2)}) async-start(), calls=%async_computation.8 | async-start | bytes 2621440 | tf_op jit(solution)/shard_map/psum | solution.py:12
  491.4 248.7 %reduce-scatter.5.cloned.1.call-start = ((), (), s32[]{:S(2)}) async-start(), calls=%async_computation.9 | async-start | bytes 1392640 | tf_op jit(solution)/shard_map/reduce_scatter | solution.py:72
  608.8 9.9 %copy-start.3 = (f32[2,128,1280]{2,1,0:T(8,128)S(1)}, f32[2,128,1280]{2,1,0:T(8,128)}, u32[]{:S(2)}) copy-start(f32[2,128,1280]{2,1,0:T(8,128)} %all-reduce.8.cloned.1.call-done) | copy-start | bytes 3932164
  618.7 19.8 %slice-start.2 = ((s8[6553600]{0:T(1024)(128)(4,1)}), s8[4194304]{0:T(1024)(128)(4,1)S(1)}, s32[]{:S(2)}) async-start(s8[6553600]{0:T(1024)(128)(4,1)} %bitcast.62), calls=%async_computation.12 | async-start | bytes 8388608
  628.5 10.1 %slice-start.3 = ((s8[6553600]{0:T(1024)(128)(4,1)}), s8[2359296]{0:T(1024)(128)(4,1)S(1)}, s32[]{:S(2)}) async-start(s8[6553600]{0:T(1024)(128)(4,1)} %bitcast.62), calls=%async_computation.13 | async-start | bytes 4718592
  646.5 93.5 %copy-start.5 = (f32[2,8,1280]{2,1,0:T(8,128)S(1)}, f32[2,8,1280]{2,1,0:T(8,128)}, u32[]{:S(2)}) copy-start(f32[2,8,1280]{2,1,0:T(8,128)} %reduce-scatter.3.cloned.1.call-done) | copy-start | bytes 245764
Sparse Core Ops, SparseCore 0:
  9.8 65.3 all-gather.1
  77.8 118.1 all-reduce.5
  198.7 126.2 all-reduce.3
  357.0 93.2 reduce-scatter.2
  491.5 117.2 all-reduce.7
  646.7 93.2 reduce-scatter.4
